TPU v7x, 512 devices: a whole 4x4x16 slice. The times are simulated.
512 devices in a mesh: cfg: 2 (over x_lo), seq: 256 (over y, x_hi, z, core).
Axes of the slice: x: 4 (x_hi: 2, x_lo: 2; x = x_hi * 2 + x_lo), y: 4, z: 16, core: 2. Of those that a mesh axis runs over, the one named last changes fastest.
Arguments:
- img_queries: bfloat16 [2, 3072, 1216], P('cfg', 'seq')
- img_keys: bfloat16 [2, 3072, 1216], P('cfg', 'seq')
- img_values: bfloat16 [2, 3072, 1216], P('cfg', 'seq'), may hold values from -6 to 6
- text_keys: bfloat16 [2, 256, 1216], P('cfg', 'seq'), may hold values from -6 to 6
- text_values: bfloat16 [2, 256, 1216], P('cfg', 'seq'), may hold values from -18 to 18
- query_gain: float32 [64], replicated, may hold values from 0.5 to 8, as said below
- key_gain: float32 [64], replicated, may hold values from 0.5 to 8, as said below
- text_gain: float32 [64], replicated, may hold values from 0.5 to 8, as said below
- text_lengths: int32 [2], P('cfg'), may hold values from 1 to 256, as said below
- text_blocks: int32 [2, 256], P('cfg', 'seq'), may hold values from 0 to 1
- latent: float32 [3072, 64], P('seq', 'cfg'), may hold values from -6 to 6
- base_velocity: bfloat16 [2, 3072, 64], P('cfg', 'seq'), may hold values from -6 to 6
- out_weight: bfloat16 [1216, 64], replicated, may hold values from -1.25 to 1.25
- timestep: int32 [1], replicated, may hold values from 0 to 27
Outputs:
- next_latent: float32 [3072, 64], P('seq', 'cfg')
- denoised: float32 [3072, 64], P('seq', 'cfg')
Inputs may be any that keep to these rules, and one draw needn't show every extreme that they name: `query_gain`: gains are positive. `key_gain`: gains are positive. `text_gain`: gains are positive. `text_lengths`: one of the two halves has all 256 slots within its length.
All inputs are finite; a program needn't handle non-finite values.
Results may differ from a plain program's by a relative error of at most 0.007.
The roundings to bfloat16 on the way count: a program that leaves them out, or rounds other values in their place, can miss the bound.
Values may be sent and summed in bfloat16 or wider, within the bound.
No kernel may reach another device: no remote copies, remote signals or barrier semaphores. Data moves between devices by JAX's collectives and lax.ppermute only.
A program may use at most 128 MiB of HBM per device.

v0:
```python
import math
import jax
import jax.numpy as jnp
from jax import lax
from jax.sharding import PartitionSpec as P

STEPS = 28
epsilon = 1e-06
guidance = 3.5
shift_factor = 3.0
masked_score = -1e30


def from_partner(block, axis, stride):
    count = lax.axis_size(axis)
    route = []
    for low in range(count):
        high = low | 1 << stride
        if high != low and high < count:
            route += [(low, high), (high, low)]
    return lax.ppermute(block, axis, route)


def head_norm(values, gain_row):
    widened = values.astype(jnp.float32).reshape(values.shape[0], -1, gain_row.shape[0])
    scaled = (
        widened
        * lax.rsqrt(jnp.mean(widened * widened, axis=-1, keepdims=True) + epsilon)
        * gain_row
    )
    return scaled.astype(jnp.bfloat16)


def sigma_at(position):
    time_left = 1.0 - position / STEPS
    return shift_factor * time_left / (1.0 + (shift_factor - 1.0) * time_left)


def attend_block(running, queries, keys_block, values_block, usable):
    run_max, run_total, run_sum = running
    head_count = queries.shape[1]
    head_size = queries.shape[2]
    keys_heads = keys_block.reshape(keys_block.shape[0], head_count, head_size)
    values_heads = values_block.reshape(values_block.shape[0], head_count, head_size)
    scores = jnp.einsum("rhd,khd->hrk", queries, keys_heads, preferred_element_type=jnp.float32) * (
        1.0 / math.sqrt(head_size)
    )
    scores = jnp.where(usable[None, None, :], scores, masked_score)
    new_max = jnp.maximum(run_max, jnp.max(scores, axis=-1))
    factor = jnp.exp(run_max - new_max)
    weights_block = jnp.where(usable[None, None, :], jnp.exp(scores - new_max[..., None]), 0.0)
    run_total = run_total * factor + jnp.sum(weights_block, axis=-1)
    run_sum = run_sum * factor[..., None] + jnp.einsum(
        "hrk,khd->hrd",
        weights_block.astype(jnp.bfloat16),
        values_heads,
        preferred_element_type=jnp.float32,
    )
    return (new_max, run_total, run_sum)


def attend_text(running, queries, keys_block, values_block, usable_flags):
    usable = usable_flags == 1

    def take_block(state_in):
        return attend_block(state_in, queries, keys_block, values_block, usable)

    def keep_state(state_in):
        return state_in

    return lax.cond(jnp.any(usable), take_block, keep_state, running)


def on_device(
    img_queries,
    img_keys,
    img_values,
    text_keys,
    text_values,
    query_gain,
    key_gain,
    text_gain,
    text_lengths,
    text_blocks,
    latent,
    base_velocity,
    out_weight,
    timestep,
):
    head_size = query_gain.shape[0]
    head_count = img_queries.shape[2] // head_size
    row_count = img_queries.shape[1]
    text_count = text_keys.shape[1]
    queries = head_norm(img_queries[0], query_gain)
    keys_local = head_norm(img_keys[0], key_gain).reshape(row_count, head_count * head_size)
    values_local = img_values[0]
    text_keys_local = head_norm(text_keys[0], text_gain).reshape(text_count, head_count * head_size)
    text_values_local = text_values[0]
    slot_index = lax.axis_index("seq") * text_count + jnp.arange(text_count, dtype=jnp.int32)
    usable_text = ((slot_index < text_lengths[0]) & (text_blocks[0, 0] == 1)).astype(jnp.int32)
    initial = (
        jnp.full((head_count, row_count), masked_score, jnp.float32),
        jnp.zeros((head_count, row_count), jnp.float32),
        jnp.zeros((head_count, row_count, head_size), jnp.float32),
    )
    running = initial
    key_piece = lax.all_gather(keys_local, "seq", axis=0, tiled=True)
    value_piece = lax.all_gather(values_local, "seq", axis=0, tiled=True)
    text_key_piece = lax.all_gather(text_keys_local, "seq", axis=0, tiled=True)
    text_value_piece = lax.all_gather(text_values_local, "seq", axis=0, tiled=True)
    usable_piece = lax.all_gather(usable_text, "seq", axis=0, tiled=True)
    every_key = jnp.ones((key_piece.shape[0],), dtype=jnp.bool_)
    running = attend_block(running, queries, key_piece, value_piece, every_key)
    final_state = attend_text(running, queries, text_key_piece, text_value_piece, usable_piece)
    run_max, run_total, run_sum = final_state
    attended = (
        (run_sum / run_total[..., None])
        .transpose(1, 0, 2)
        .reshape(row_count, head_count * head_size)
        .astype(jnp.bfloat16)
    )
    velocity = base_velocity[0].astype(jnp.float32) + jnp.dot(
        attended, out_weight, preferred_element_type=jnp.float32
    )
    guide_half = lax.axis_index("cfg")
    half_width = latent.shape[1]
    own_part = lax.dynamic_slice_in_dim(velocity, guide_half * half_width, half_width, 1)
    sent_part = lax.dynamic_slice_in_dim(velocity, (1 - guide_half) * half_width, half_width, 1)
    partner = from_partner(sent_part, "cfg", 0)
    cond_part = jnp.where(guide_half == 0, own_part, partner)
    uncond_part = jnp.where(guide_half == 0, partner, own_part)
    guided = uncond_part + guidance * (cond_part - uncond_part)
    step_now = timestep[0].astype(jnp.float32)
    sigma_now = sigma_at(step_now)
    sigma_next = sigma_at(step_now + 1.0)
    next_latent = latent + (sigma_next - sigma_now) * guided
    denoised = latent - sigma_now * guided
    return (next_latent, denoised)


def solution(mesh):
    return jax.shard_map(
        on_device,
        mesh=mesh,
        in_specs=(
            P("cfg", "seq", None),
            P("cfg", "seq", None),
            P("cfg", "seq", None),
            P("cfg", "seq", None),
            P("cfg", "seq", None),
            P(),
            P(),
            P(),
            P("cfg"),
            P("cfg", "seq"),
            P("seq", "cfg"),
            P("cfg", "seq", None),
            P(),
            P(),
        ),
        out_specs=(P("seq", "cfg"), P("seq", "cfg")),
        check_vma=False,
    )
```

profile of v0, /device:TPU:1, one launch (start us, length us, event | category | flops | bytes accessed | tf_op | source)
XLA Modules:
  0.0 1482.1 jit_solution(14273524936408419100)
XLA Ops:
  7.2 0.8 convert_multiply_fusion
  8.5 0.7 mul.197
  9.2 1.4 fusion.27
  10.7 1.4 copy.44
  13.4 1.3 dynamic-slice
  14.7 0.7 fusion.33
  15.5 655.9 %all-reduce = s32[256]{0:T(256)S(1)} all-reduce(s32[256]{0:T(256)S(1)} %fusion.33), channel_id=1, replica_groups=mesh['cfg'=2,'seq'=256] {'seq'}, use_global_device_ids=true, to_apply=%add | all-reduce | flops 256 | bytes 2048
  671.3 0.6 fusion.35
  672.6 0.9 reshape.183
  673.5 0.7 mul.209
  674.2 0.7 fusion.31
  675.0 0.1 reduce_sum.48
  675.3 0.7 fusion.30
  676.0 358.8 %all-gather.3 = bf16[256,1,1216]{2,1,0:T(2,128)(2,1)S(1)} all-gather(bf16[1,1,1216]{2,1,0:T(2,128)(2,1)S(1)} %fusion.30), channel_id=1, replica_groups=mesh['cfg'=2,'seq'=256] {'seq'}, dimensions={0}, use_global_device_ids=true | all-gather | bytes 625024 | tf_op jit(solution)/shard_map/all_gather | solution.py:109
  1034.8 1.3 copy.46
  1036.1 353.9 %all-gather.1 = bf16[256,1,1216]{2,1,0:T(2,128)(2,1)S(1)} all-gather(bf16[1,1,1216]{2,1,0:T(2,128)(2,1)S(1)} %copy-done.2), channel_id=3, replica_groups=mesh['cfg'=2,'seq'=256] {'seq'}, dimensions={0}, use_global_device_ids=true | all-gather | bytes 625024 | tf_op jit(solution)/shard_map/all_gather | solution.py:110
  1389.9 1.3 copy.47
  1391.5 24.8 %reshape.174 = bf16[3072,19,64]{2,1,0:T(8,128)(2,1)} reshape(bf16[256,12,1216]{2,1,0:T(8,128)(2,1)} %all-gather.9.cloned.1.call-done) | data formatting | bytes 14942208 | tf_op jit(solution)/shard_map/reshape | solution.py:43
  1416.3 12.3 fusion.37
  1428.5 2.7 fusion.15
  1431.3 31.0 %copy.45 = bf16[1,3072,1216]{1,2,0:T(8,128)(2,1)} copy(bf16[1,3072,1216]{2,0,1:T(2,128)(2,1)} %all-gather.7.cloned.1.call-done) | data formatting | bytes 14942208 | tf_op jit(solution)/shard_map/all_gather | solution.py:108
  1462.3 6.4 fusion.19
  1468.7 0.9 conditional.1
  1468.8 0.3 fusion.36
  1469.1 0.2 fusion.2
  1469.3 0.3 convolution_add_fusion
  1469.6 0.1 fusion.26
  1469.8 0.1 convert_element_type.127
  1469.9 0.2 convolution_add_fusion.1
  1470.2 2.2 collective-permute-start
  1473.2 1.4 collective-permute-done
  1474.6 0.7 multiply_subtract_fusion
  (37 shorter events, 1.3 us)
Async XLA Ops:
  7.2 1462.7 %copy-start = (bf16[1216,64]{0,1:T(8,128)(2,1)S(1)}, bf16[1216,64]{0,1:T(8,128)(2,1)}, u32[]{:S(2)}) copy-start(bf16[1216,64]{0,1:T(8,128)(2,1)} %param.28) | copy-start | bytes 466948
  7.2 1028.9 %copy-start.2 = (bf16[1,1,1216]{2,1,0:T(2,128)(2,1)S(1)}, bf16[1,1,1216]{2,1,0:T(2,128)(2,1)}, u32[]{:S(2)}) copy-start(bf16[1,1,1216]{2,1,0:T(2,128)(2,1)} %param.20) | copy-start | bytes 7300
  7.2 1384.3 %all-gather.9.cloned.1.call-start = ((), (), s32[]{:S(2)}) async-start(), calls=%async_computation.1 | async-start | bytes 10526720 | tf_op jit(solution)/shard_map/all_gather | solution.py:107
  8.4 1382.9 %copy-start.4 = (f32[64]{0:T(128)S(1)}, f32[64]{0:T(128)}, u32[]{:S(2)}) copy-start(f32[64]{0:T(128)} %param.21) | copy-start | bytes 772
  10.6 1420.7 %all-gather.7.cloned.1.call-start = ((), (), s32[]{:S(2)}) async-start(), calls=%async_computation | async-start | bytes 15790080 | tf_op jit(solution)/shard_map/all_gather | solution.py:108
  1462.3 7.6 copy-start.3
  1462.3 12.2 copy-start.1
  1470.2 4.4 collective-permute-start
Sparse Core Ops, SparseCore 0:
  12.5 234.6 all-gather.8
  252.0 238.5 all-gather.6
where the time goes:
time: 1480 us
  blocking collectives  1370 us (93%)
  local copies, waits for them, and re-layouts  64.1 us (4%)
  matrix products  19.4 us (1%)
  between operations  16.9 us (1%)
    unnamed x1, blocking collectives  656 us
    all_gather x1, blocking collectives, on_device(): text_key_piece = lax.all_gather(text_keys_local, 'seq', axis=0, tiled=True)  359 us
    all_gather x1, blocking collectives, on_device(): lax.all_gather(text_values_local, 'seq', axis=0, tiled=True)  354 us
    all_gather x1, local copies, waits for them, and re-layouts, on_device(): value_piece = lax.all_gather(values_local, 'seq', axis=0, tiled=True)  31 us
  transfers between devices with their start and end apart: 3, of which 1 were waited for; matrix products, arithmetic and copies ran while one was open for 3% of the time, Pallas kernels for 0%

commit v1 on v0

--- a/solution.py
+++ b/solution.py
@@ -9,6 +9,13 @@
 guidance = 3.5
 shift_factor = 3.0
 masked_score = -1e30
+
+
+def place_the_widths(vector):
+    mixed_arr = jnp.concatenate(
+        lax.all_to_all(jnp.stack(lax.axis_size("seq") * [vector], axis=0), "seq", 0, 0), axis=0
+    )
+    return mixed_arr
 
 
 def from_partner(block, axis, stride):
@@ -107,7 +114,7 @@
     key_piece = lax.all_gather(keys_local, "seq", axis=0, tiled=True)
     value_piece = lax.all_gather(values_local, "seq", axis=0, tiled=True)
     text_key_piece = lax.all_gather(text_keys_local, "seq", axis=0, tiled=True)
-    text_value_piece = lax.all_gather(text_values_local, "seq", axis=0, tiled=True)
+    text_value_piece = place_the_widths(text_values_local)
     usable_piece = lax.all_gather(usable_text, "seq", axis=0, tiled=True)
     every_key = jnp.ones((key_piece.shape[0],), dtype=jnp.bool_)
     running = attend_block(running, queries, key_piece, value_piece, every_key)

time: 1480 us -> 1170 us (0.79)
  blocking collectives: 1370 us -> 1020 us
  starting transfers between devices: 2.33 us -> 27.2 us
    all_gather x1 -> x0, blocking collectives: 354 us -> none  [on_device(): lax.all_gather(text_values_local, 'seq', axis=0, tiled=True)]
    all_to_all x0 -> x1, starting transfers between devices: none -> 24.5 us  [place_the_widths(): lax.all_to_all(jnp.stack(lax.axis_size('seq') * [vector], axis=0), 'seq',...]
  transfers between devices with their start and end apart: 3 -> 4, of which waited for: 1 -> 1; matrix products, arithmetic and copies ran while one was open for 3% -> 5% of each run, Pallas kernels for 0% -> 0%
where the time goes in v1:
time: 1170 us
  blocking collectives  1020 us (87%)
  local copies, waits for them, and re-layouts  66.5 us (6%)
  starting transfers between devices  27.2 us (2%)
  matrix products  19.4 us (2%)
  between operations  17 us (1%)
  other arithmetic  13.4 us (1%)
    unnamed x1, blocking collectives  668 us
    all_gather x1, blocking collectives, on_device(): text_key_piece = lax.all_gather(text_keys_local, 'seq', axis=0, tiled=True)  353 us
    all_gather x1, local copies, waits for them, and re-layouts, on_device(): value_piece = lax.all_gather(values_local, 'seq', axis=0, tiled=True)  31 us
    reshape x1, local copies, waits for them, and re-layouts, attend_block(): keys_heads = keys_block.reshape(keys_block.shape[0], head_count, head_size)  24.8 us
    all_to_all x1, starting transfers between devices, place_the_widths(): lax.all_to_all(jnp.stack(lax.axis_size('seq') * [vector], axis=0), 'seq',...  24.5 us
  transfers between devices with their start and end apart: 4, of which 1 were waited for; matrix products, arithmetic and copies ran while one was open for 5% of the time, Pallas kernels for 0%

profile of v1, /device:TPU:1, one launch (start us, length us, event | category | flops | bytes accessed | tf_op | source)
XLA Modules:
  0.0 1165.1 jit_solution(10318169095163260236)
XLA Ops:
  7.3 0.8 convert_multiply_fusion
  8.5 0.7 mul.197
  9.2 1.4 fusion.27
  10.7 1.4 copy.41
  12.2 0.7 reduce.3
  12.9 0.7 stack.3
  13.6 0.5 broadcast.103
  14.1 4.8 reduce.5
  18.9 1.5 reshape.204
  20.4 24.5 %all-to-all-start = ((bf16[256,2,608]{2,1,0:T(2,128)(2,1)}), bf16[256,2,608]{2,1,0:T(2,128)(2,1)S(1)}, u32[]{:S(2)}, u32[]{:S(2)}) async-start(bf16[256,2,608]{2,1,0:T(2,128)(2,1)} %reshape.204), calls=%async_computation | async-start | bytes 1310720 | tf_op jit(solution)/shard_map/all_to_all | solution.py:16
  46.3 1.3 dynamic-slice
  47.5 0.7 fusion.33
  48.3 667.6 %all-reduce = s32[256]{0:T(256)S(1)} all-reduce(s32[256]{0:T(256)S(1)} %fusion.33), channel_id=1, replica_groups=mesh['cfg'=2,'seq'=256] {'seq'}, use_global_device_ids=true, to_apply=%add | all-reduce | flops 256 | bytes 2048
  715.9 0.6 fusion.35
  717.8 352.8 %all-gather.2 = bf16[256,1,1216]{2,1,0:T(2,128)(2,1)S(1)} all-gather(bf16[1,1,1216]{2,1,0:T(2,128)(2,1)S(1)} %fusion.30), channel_id=1, replica_groups=mesh['cfg'=2,'seq'=256] {'seq'}, dimensions={0}, use_global_device_ids=true | all-gather | bytes 625024 | tf_op jit(solution)/shard_map/all_gather | solution.py:116
  1070.6 1.3 copy.43
  1072.1 1.1 reshape.205
  1073.2 24.8 %reshape.174 = bf16[3072,19,64]{2,1,0:T(8,128)(2,1)} reshape(bf16[256,12,1216]{2,1,0:T(8,128)(2,1)} %all-gather.8.cloned.1.call-done) | data formatting | bytes 14942208 | tf_op jit(solution)/shard_map/reshape | solution.py:50
  1098.0 12.3 %fusion.37 = (f32[19,12]{1,0:T(8,128)S(1)}, f32[19,12,3072]{2,1,0:T(8,128)}) fusion(bf16[3072,19,64]{2,1,0:T(8,128)(2,1)} %reshape.174, bf16[12,19,64]{2,1,0:T(8,128)(2,1)S(1)} %multiply_convert_fusion), kind=kOutput, calls=%fused_computation.56 | convolution fusion | flops 91053856 | bytes 10302864 | tf_op jit(solution)/shard_map/rhd,khd->hrk/dot_general | solution.py:52
  1110.2 2.7 fusion.15
  1113.0 31.0 %copy.42 = bf16[1,3072,1216]{1,2,0:T(8,128)(2,1)} copy(bf16[1,3072,1216]{2,0,1:T(2,128)(2,1)} %all-gather.6.cloned.1.call-done) | data formatting | bytes 14942208 | tf_op jit(solution)/shard_map/all_gather | solution.py:115
  1144.1 6.4 fusion.19
  1150.5 2.2 conditional.1
  1150.5 0.3 fusion.36
  1150.8 0.2 fusion.2
  1151.0 1.3 copy.45
  1152.3 0.3 convolution_add_fusion
  1152.6 0.1 fusion.26
  1152.9 0.2 convolution_add_fusion.1
  1153.2 2.6 collective-permute-start
  1156.5 1.1 collective-permute-done
  1157.6 0.7 multiply_subtract_fusion
  (48 shorter events, 1.7 us)
Async XLA Ops:
  7.2 1145.8 %copy-start = (bf16[1216,64]{0,1:T(8,128)(2,1)S(1)}, bf16[1216,64]{0,1:T(8,128)(2,1)}, u32[]{:S(2)}) copy-start(bf16[1216,64]{0,1:T(8,128)(2,1)} %param.28) | copy-start | bytes 466948
  7.2 710.0 %copy-start.1 = (bf16[1,12,1216]{2,1,0:T(8,128)(2,1)S(1)}, bf16[1,12,1216]{2,1,0:T(8,128)(2,1)}, u32[]{:S(2)}) copy-start(bf16[1,12,1216]{2,1,0:T(8,128)(2,1)} %param.16) | copy-start | bytes 87556
  7.2 710.1 %copy-start.6 = (f32[64]{0:T(128)S(1)}, f32[64]{0:T(128)}, u32[]{:S(2)}) copy-start(f32[64]{0:T(128)} %param.23) | copy-start | bytes 772
  7.2 710.2 %copy-start.2 = (bf16[1,1,1216]{2,1,0:T(2,128)(2,1)S(1)}, bf16[1,1,1216]{2,1,0:T(2,128)(2,1)}, u32[]{:S(2)}) copy-start(bf16[1,1,1216]{2,1,0:T(2,128)(2,1)} %param.19) | copy-start | bytes 7300
  7.2 1066.0 %all-gather.8.cloned.1.call-start = ((), (), s32[]{:S(2)}) async-start(), calls=%async_computation.2 | async-start | bytes 10526720 | tf_op jit(solution)/shard_map/all_gather | solution.py:114
  10.7 1102.4 %all-gather.6.cloned.1.call-start = ((), (), s32[]{:S(2)}) async-start(), calls=%async_computation.1 | async-start | bytes 15790080 | tf_op jit(solution)/shard_map/all_gather | solution.py:115
  14.1 1057.9 %copy-start.5 = (f32[64]{0:T(128)S(1)}, f32[64]{0:T(128)}, u32[]{:S(2)}) copy-start(f32[64]{0:T(128)} %param.21) | copy-start | bytes 772
  20.4 1051.7 %all-to-all-start = ((bf16[256,2,608]{2,1,0:T(2,128)(2,1)}), bf16[256,2,608]{2,1,0:T(2,128)(2,1)S(1)}, u32[]{:S(2)}, u32[]{:S(2)}) async-start(bf16[256,2,608]{2,1,0:T(2,128)(2,1)} %reshape.204), calls=%async_computation | async-start | bytes 1310720 | tf_op jit(solution)/shard_map/all_to_all | solution.py:16
  1150.4 2.5 copy-start.4
  1150.4 7.1 copy-start.3
  1153.2 4.4 collective-permute-start
Sparse Core Ops, SparseCore 0:
  12.5 235.9 all-gather.7
  253.2 238.8 all-gather.5
